TPU v7x, 32 devices: a whole 2x2x4 slice. The times are simulated.
32 devices in a mesh: dp: 8 (over y, x, core), seg: 4 (over z).
Axes of the slice: x: 2, y: 2, z: 4, core: 2. Of those that a mesh axis runs over, the one named last changes fastest.
Arguments:
- tokens: bfloat16 [2, 16, 2048, 768], P(None, 'dp', 'seg'), may hold values from -6 to 6
- cotangent: bfloat16 [2, 16, 2048, 768], P(None, 'dp', 'seg'), may hold values from -6 to 6
- document_ids: int32 [2, 16, 16], P(None, 'dp'), may hold values from 0 to 3, never falling along the last dimension, each value on 1 to 8 neighbouring positions
- position_ids: int32 [2, 16, 16], P(None, 'dp'), may hold values from 0 to 63
- project_in: bfloat16 [2, 768, 2304], P(None, 'dp', 'seg'), may hold values from -0.3125 to 0.3125
- project_out: bfloat16 [2, 768, 768], P(None, 'dp', 'seg'), may hold values from -0.875 to 0.875
- up_weight: bfloat16 [2, 768, 3072], P(None, 'dp', 'seg'), may hold values from -0.21875 to 0.21875
- down_weight: bfloat16 [2, 3072, 768], P(None, 'dp', 'seg'), may hold values from -0.109375 to 0.109375
- norm_gains: bfloat16 [2, 768, 2], P(None, 'dp'), may hold values from 0.5 to 1.5
- biases: bfloat16 [2, 768, 6], P(None, 'dp'), may hold values from -1.25 to 1.25
- up_bias: bfloat16 [2, 3072], P(None, 'dp'), may hold values from -1.25 to 1.25
- position_table: bfloat16 [768, 64], P('dp'), may hold values from -3 to 3
Outputs:
- layer_out: bfloat16 [2, 16, 2048, 768], P(None, 'dp', 'seg')
- input_grad: float32 [2, 16, 2048, 768], P(None, 'dp', 'seg')
- project_in_grad: float32 [2, 768, 2304], P(None, 'dp', 'seg')
- project_out_grad: float32 [2, 768, 768], P(None, 'dp', 'seg')
- up_weight_grad: float32 [2, 768, 3072], P(None, 'dp', 'seg')
- down_weight_grad: float32 [2, 3072, 768], P(None, 'dp', 'seg')
- norm_gains_grad: float32 [2, 768, 2], P(None, 'dp')
- biases_grad: float32 [2, 768, 6], P(None, 'dp')
- up_bias_grad: float32 [2, 3072], P(None, 'dp')
- position_table_grad: float32 [768, 64], P('dp')
Inputs may be any that keep to these rules, and one draw needn't show every extreme that they name: `document_ids`: document ids count from 0 in every row and never fall along it; a document has 1 to 8 segments.
All inputs are finite; a program needn't handle non-finite values.
Results may differ from a plain program's by a relative error of at most 0.028.
Values may be sent and summed in bfloat16 or wider, within the bound.
A program may use at most 320 MiB of HBM per device.

v0:
```python
import jax
import jax.numpy as jnp
from jax import lax
from jax.sharding import PartitionSpec as P

HEADS = 12
HD = 64
SEGLEN = 128
POS = 64
NORM_EPS = 1e-05
PRECISE = lax.Precision.HIGHEST


def norm_apply(inputs, norm_gain, norm_shift):
    average = jnp.mean(inputs, axis=-1, keepdims=True)
    centered = inputs - average
    variance = jnp.mean(centered * centered, axis=-1, keepdims=True)
    return centered * lax.rsqrt(variance + NORM_EPS) * norm_gain + norm_shift


def norm_backward(inputs, norm_gain, norm_shift, upstream):
    unused_out, pull_back = jax.vjp(norm_apply, inputs, norm_gain, norm_shift)
    return pull_back(upstream)


def gelu_exact(inputs):
    return jax.nn.gelu(inputs, approximate=False)


def soft_scores(queries, key_rows, same_document):
    scores = jnp.einsum(
        "gqhe,gkhe->ghqk", queries, key_rows, preferred_element_type=jnp.float32
    ) * HD ** (-0.5)
    if same_document is not None:
        scores = jnp.where(same_document[:, None, :, :], scores, -1e30)
    return scores


def block_forward(source, residual, weights, same_document):
    project_in, project_out, up_weight, down_weight, norm_gains, biases, up_bias = weights
    features = source.shape[-1]
    leading = source.shape[:-1]
    head_shape = leading + (HEADS, HD)
    joined = jnp.einsum("gld,de->gle", source, project_in, preferred_element_type=jnp.float32)
    queries = (joined[..., :features] + biases[:, 0]).astype(jnp.bfloat16)
    key_rows = joined[..., features : 2 * features].astype(jnp.bfloat16)
    values = (joined[..., 2 * features :] + biases[:, 1]).astype(jnp.bfloat16)
    scores = soft_scores(queries.reshape(head_shape), key_rows.reshape(head_shape), same_document)
    log_total = jax.nn.logsumexp(scores, axis=-1, keepdims=True)
    attention = jnp.exp(scores - log_total).astype(jnp.bfloat16)
    context = jnp.einsum(
        "ghqk,gkhe->gqhe", attention, values.reshape(head_shape), preferred_element_type=jnp.float32
    )
    context = context.reshape(leading + (features,)).astype(jnp.bfloat16)
    mixed_input = residual + (
        jnp.einsum("gld,de->gle", context, project_out, preferred_element_type=jnp.float32)
        + biases[:, 2]
    )
    first_norm = norm_apply(mixed_input, norm_gains[:, 0], biases[:, 4])
    first_low = first_norm.astype(jnp.bfloat16)
    pre_gelu = (
        jnp.einsum("gld,df->glf", first_low, up_weight, preferred_element_type=jnp.float32)
        + up_bias
    )
    activation = gelu_exact(pre_gelu).astype(jnp.bfloat16)
    second_input = first_norm + (
        jnp.einsum("glf,fd->gld", activation, down_weight, preferred_element_type=jnp.float32)
        + biases[:, 3]
    )
    result = norm_apply(second_input, norm_gains[:, 1], biases[:, 5])
    stored = (
        queries,
        key_rows,
        values,
        log_total,
        context,
        mixed_input,
        first_low,
        pre_gelu,
        activation,
        second_input,
    )
    return (result, stored)


def block_backward(source, stored, weights, same_document, upstream):
    project_in, project_out, up_weight, down_weight, norm_gains, biases, up_bias = weights
    (
        queries,
        key_rows,
        values,
        log_total,
        context,
        mixed_input,
        first_low,
        pre_gelu,
        activation,
        second_input,
    ) = stored
    features = source.shape[-1]
    leading = source.shape[:-1]
    head_shape = leading + (HEADS, HD)
    sum_axes = (0, 1)
    second_grad, gain_two, shift_two = norm_backward(
        second_input, norm_gains[:, 1], biases[:, 5], upstream
    )
    branch_grad = second_grad.astype(jnp.bfloat16)
    down_grad = jnp.einsum(
        "glf,gld->fd", activation, branch_grad, preferred_element_type=jnp.float32
    )
    activation_grad = jnp.einsum(
        "gld,fd->glf", branch_grad, down_weight, preferred_element_type=jnp.float32
    )
    unused_out, gelu_pull = jax.vjp(gelu_exact, pre_gelu)
    pre_gelu_grad = gelu_pull(activation_grad)[0].astype(jnp.bfloat16)
    up_grad = jnp.einsum(
        "gld,glf->df", first_low, pre_gelu_grad, preferred_element_type=jnp.float32
    )
    first_grad = second_grad + jnp.einsum(
        "glf,df->gld", pre_gelu_grad, up_weight, preferred_element_type=jnp.float32
    )
    mixed_grad, gain_one, shift_one = norm_backward(
        mixed_input, norm_gains[:, 0], biases[:, 4], first_grad
    )
    mixed_low = mixed_grad.astype(jnp.bfloat16)
    outward_grad = jnp.einsum("gld,gle->de", context, mixed_low, preferred_element_type=jnp.float32)
    context_grad = jnp.einsum(
        "gle,de->gld", mixed_low, project_out, preferred_element_type=jnp.float32
    )
    context_grad = context_grad.astype(jnp.bfloat16).reshape(head_shape)
    query_heads = queries.reshape(head_shape)
    key_heads = key_rows.reshape(head_shape)
    scores = soft_scores(query_heads, key_heads, same_document)
    attention = jnp.exp(scores - log_total)
    value_grad = jnp.einsum(
        "ghqk,gqhe->gkhe",
        attention.astype(jnp.bfloat16),
        context_grad,
        preferred_element_type=jnp.float32,
    )
    soft_grad = jnp.einsum(
        "gqhe,gkhe->ghqk",
        context_grad,
        values.reshape(head_shape),
        preferred_element_type=jnp.float32,
    )
    score_grad = attention * (soft_grad - jnp.sum(soft_grad * attention, axis=-1, keepdims=True))
    score_grad = score_grad.astype(jnp.bfloat16)
    query_grad = jnp.einsum(
        "ghqk,gkhe->gqhe", score_grad, key_heads, preferred_element_type=jnp.float32
    ) * HD ** (-0.5)
    key_grad = jnp.einsum(
        "ghqk,gqhe->gkhe", score_grad, query_heads, preferred_element_type=jnp.float32
    ) * HD ** (-0.5)
    joined_grad = jnp.concatenate(
        [
            query_grad.reshape(leading + (features,)),
            key_grad.reshape(leading + (features,)),
            value_grad.reshape(leading + (features,)),
        ],
        axis=-1,
    ).astype(jnp.bfloat16)
    inward_grad = jnp.einsum("gld,gle->de", source, joined_grad, preferred_element_type=jnp.float32)
    source_grad = mixed_grad + jnp.einsum(
        "gle,de->gld", joined_grad, project_in, preferred_element_type=jnp.float32
    )
    bias_grad = jnp.stack(
        [
            jnp.sum(joined_grad[..., :features], axis=sum_axes, dtype=jnp.float32),
            jnp.sum(joined_grad[..., 2 * features :], axis=sum_axes, dtype=jnp.float32),
            jnp.sum(mixed_low, axis=sum_axes, dtype=jnp.float32),
            jnp.sum(branch_grad, axis=sum_axes, dtype=jnp.float32),
            shift_one,
            shift_two,
        ],
        axis=-1,
    )
    gain_grad = jnp.stack([gain_one, gain_two], axis=-1)
    bias_up_grad = jnp.sum(pre_gelu_grad, axis=sum_axes, dtype=jnp.float32)
    return (
        source_grad,
        (inward_grad, outward_grad, up_grad, down_grad, gain_grad, bias_grad, bias_up_grad),
    )


def pick_block(weights, which_block):
    return (
        weights[0][which_block],
        weights[1][which_block],
        weights[2][which_block],
        weights[3][which_block],
        weights[4][which_block].astype(jnp.float32),
        weights[5][which_block].astype(jnp.float32),
        weights[6][which_block].astype(jnp.float32),
    )


def shards(
    tokens,
    cotangent,
    document_ids,
    position_ids,
    project_in,
    project_out,
    up_weight,
    down_weight,
    norm_gains,
    biases,
    up_bias,
    position_table,
):
    shard_index = lax.axis_index("seg")
    first_shard = (shard_index == 0).astype(jnp.float32)
    micro_count, row_count, row_tokens, features = tokens.shape
    segment_count = row_tokens // SEGLEN
    group_count = row_count * segment_count
    slot_ids = jnp.arange(POS, dtype=jnp.int32)
    outputs = []
    input_grads = []
    totals = None
    for micro_step in range(micro_count):
        weights = (
            lax.all_gather(
                lax.all_gather(project_in, "seg", axis=2, tiled=True), "dp", axis=1, tiled=True
            ),
            lax.all_gather(
                lax.all_gather(project_out, "seg", axis=2, tiled=True), "dp", axis=1, tiled=True
            ),
            lax.all_gather(
                lax.all_gather(up_weight, "seg", axis=2, tiled=True), "dp", axis=1, tiled=True
            ),
            lax.all_gather(
                lax.all_gather(down_weight, "seg", axis=2, tiled=True), "dp", axis=1, tiled=True
            ),
            lax.all_gather(norm_gains, "dp", axis=1, tiled=True),
            lax.all_gather(biases, "dp", axis=1, tiled=True),
            lax.all_gather(up_bias, "dp", axis=1, tiled=True),
            lax.all_gather(position_table, "dp", axis=0, tiled=True),
        )
        local_weights = pick_block(weights, 0)
        cross_weights = pick_block(weights, 1)
        gathered_table = weights[7]
        segments = tokens[micro_step].reshape(group_count, SEGLEN, features)
        local_out, local_stored = block_forward(
            segments, segments.astype(jnp.float32), local_weights, None
        )
        class_own = (
            local_out[:, 0, :].astype(jnp.bfloat16).reshape(row_count, segment_count, features)
        )
        class_rows = lax.all_gather(class_own, "seg", axis=1, tiled=True)
        one_hot = (position_ids[micro_step][:, :, None] == slot_ids).astype(jnp.bfloat16)
        cross_in = class_rows.astype(jnp.float32) + jnp.einsum(
            "rsp,dp->rsd", one_hot, gathered_table, preferred_element_type=jnp.float32
        )
        documents = document_ids[micro_step]
        same_document = documents[:, :, None] == documents[:, None, :]
        cross_low = cross_in.astype(jnp.bfloat16)
        cross_out, cross_stored = block_forward(cross_low, cross_in, cross_weights, same_document)
        cross_own = lax.dynamic_slice_in_dim(
            cross_out, shard_index * segment_count, segment_count, 1
        )
        merged = local_out.at[:, 0, :].set(cross_own.reshape(group_count, features))
        outputs.append(merged.astype(jnp.bfloat16).reshape(row_count, row_tokens, features))
        weights = (
            lax.all_gather(
                lax.all_gather(project_in, "seg", axis=2, tiled=True), "dp", axis=1, tiled=True
            ),
            lax.all_gather(
                lax.all_gather(project_out, "seg", axis=2, tiled=True), "dp", axis=1, tiled=True
            ),
            lax.all_gather(
                lax.all_gather(up_weight, "seg", axis=2, tiled=True), "dp", axis=1, tiled=True
            ),
            lax.all_gather(
                lax.all_gather(down_weight, "seg", axis=2, tiled=True), "dp", axis=1, tiled=True
            ),
            lax.all_gather(norm_gains, "dp", axis=1, tiled=True),
            lax.all_gather(biases, "dp", axis=1, tiled=True),
            lax.all_gather(up_bias, "dp", axis=1, tiled=True),
            lax.all_gather(position_table, "dp", axis=0, tiled=True),
        )
        local_weights = pick_block(weights, 0)
        cross_weights = pick_block(weights, 1)
        upstream = cotangent[micro_step].reshape(group_count, SEGLEN, features)
        class_grad_own = upstream[:, 0, :].reshape(row_count, segment_count, features)
        class_grads = lax.all_gather(class_grad_own, "seg", axis=1, tiled=True)
        cross_grad, cross_terms = block_backward(
            cross_low, cross_stored, cross_weights, same_document, class_grads.astype(jnp.float32)
        )
        table_grad = jnp.einsum(
            "rsd,rsp->dp", cross_grad, one_hot.astype(jnp.float32), precision=PRECISE
        )
        own_grad = lax.dynamic_slice_in_dim(
            cross_grad, shard_index * segment_count, segment_count, 1
        )
        local_upstream = (
            upstream.astype(jnp.float32).at[:, 0, :].set(own_grad.reshape(group_count, features))
        )
        token_grad, local_terms = block_backward(
            segments, local_stored, local_weights, None, local_upstream
        )
        input_grads.append(token_grad.reshape(row_count, row_tokens, features))
        gradients = tuple(
            (
                jnp.stack([local_term, cross_term * first_shard])
                for local_term, cross_term in zip(local_terms, cross_terms)
            )
        ) + (table_grad * first_shard,)
        small_sums = lax.psum(
            (
                lax.psum_scatter(
                    gradients[4].astype(jnp.bfloat16), "dp", scatter_dimension=1, tiled=True
                ).astype(jnp.float32),
                lax.psum_scatter(
                    gradients[5].astype(jnp.bfloat16), "dp", scatter_dimension=1, tiled=True
                ).astype(jnp.float32),
                lax.psum_scatter(
                    gradients[6].astype(jnp.bfloat16), "dp", scatter_dimension=1, tiled=True
                ).astype(jnp.float32),
                lax.psum_scatter(
                    gradients[7].astype(jnp.bfloat16), "dp", scatter_dimension=0, tiled=True
                ).astype(jnp.float32),
            ),
            "seg",
        )
        reduced = (
            lax.psum_scatter(
                lax.psum_scatter(
                    gradients[0].astype(jnp.bfloat16), "dp", scatter_dimension=1, tiled=True
                ),
                "seg",
                scatter_dimension=2,
                tiled=True,
            ).astype(jnp.float32),
            lax.psum_scatter(
                lax.psum_scatter(
                    gradients[1].astype(jnp.bfloat16), "dp", scatter_dimension=1, tiled=True
                ),
                "seg",
                scatter_dimension=2,
                tiled=True,
            ).astype(jnp.float32),
            lax.psum_scatter(
                lax.psum_scatter(
                    gradients[2].astype(jnp.bfloat16), "dp", scatter_dimension=1, tiled=True
                ),
                "seg",
                scatter_dimension=2,
                tiled=True,
            ).astype(jnp.float32),
            lax.psum_scatter(
                lax.psum_scatter(
                    gradients[3].astype(jnp.bfloat16), "dp", scatter_dimension=1, tiled=True
                ),
                "seg",
                scatter_dimension=2,
                tiled=True,
            ).astype(jnp.float32),
            small_sums[0],
            small_sums[1],
            small_sums[2],
            small_sums[3],
        )
        totals = (
            reduced
            if totals is None
            else tuple((jnp.add(earlier, current) for earlier, current in zip(totals, reduced)))
        )
    return (
        jnp.stack(outputs),
        jnp.stack(input_grads),
        totals[0],
        totals[1],
        totals[2],
        totals[3],
        totals[4],
        totals[5],
        totals[6],
        totals[7],
    )


def solution(mesh):
    placed = (
        P(None, "dp", "seg", None),
        P(None, "dp", "seg", None),
        P(None, "dp", None),
        P(None, "dp", None),
        P(None, "dp", "seg"),
        P(None, "dp", "seg"),
        P(None, "dp", "seg"),
        P(None, "dp", "seg"),
        P(None, "dp", None),
        P(None, "dp", None),
        P(None, "dp"),
        P("dp", None),
    )
    return jax.shard_map(
        shards,
        mesh=mesh,
        in_specs=placed,
        out_specs=(
            P(None, "dp", "seg", None),
            P(None, "dp", "seg", None),
            P(None, "dp", "seg"),
            P(None, "dp", "seg"),
            P(None, "dp", "seg"),
            P(None, "dp", "seg"),
            P(None, "dp", None),
            P(None, "dp", None),
            P(None, "dp"),
            P("dp", None),
        ),
        check_vma=False,
    )
```

profile of v0, /device:TPU:0, one launch (start us, length us, event | category | flops | bytes accessed | tf_op | source)
XLA Modules:
  0.0 1764.4 jit_solution(14379314771954475680)
XLA Ops:
  11.2 41.5 %all_gather.32 = bf16[2,96,2304]{1,0,2:T(2,128)(2,1)S(1)} all-gather(bf16[2,96,576]{1,0,2:T(2,128)(2,1)S(1)} %copy.324), channel_id=1, replica_groups=mesh['dp'=8,'seg'=4] {'seg'}, dimensions={2}, use_global_device_ids=true | all-gather | bytes 1105920 | tf_op jit(solution)/shard_map/all_gather | solution.py:224
  55.3 16.7 all_gather.35
  244.1 19.6 %fusion.38 = (u8[128,3072]{1,0:T(8,128)(4,1)S(1)}, u8[128,3072]{1,0:T(8,128)(4,1)S(1)}, u8[128,3072]{1,0:T(8,128)(4,1)S(1)}, u8[128,3072]{1,0:T(8,128)(4,1)S(1)}, f32[8,128,3072]{2,1,0:T(8,128)}) fusion(f32[3072]{0:T(1024)S(1)} %bitcast.509, f32[8,128,3072]{2,1,0:T(8,128)} %fusion.42, bf16[2,768,3072]{2,1,0:T(8,128)(2,1)} %all-gather.14.cloned.1.call-done, ...), kind=kOutput, calls=%fused_computation.141 | convolution fusion | flops 4922277888 | bytes 34629632 | tf_op jit(solution)/shard_map/gld,df->glf/dot_general | solution.py:62
  263.7 61.2 %multiply_convert_fusion.1 = (bf16[8,128,3072]{2,1,0:T(8,128)(2,1)}, f32[8,128,3072]{2,1,0:T(8,128)}, bf16[8,128,3072]{2,1,0:T(8,128)(2,1)}, f32[8,128,3072]{2,1,0:T(8,128)}) fusion(f32[8,128,3072]{2,1,0:T(8,128)} %get-tuple-element.267, f32[3072]{0:T(1024)S(1)} %bitcast.510, u8[128,3072]{1,0:T(8,128)(4,1)S(1)} %get-tuple-element.109, ...), kind=kLoop, calls=%fused_computation.28 | loop fusion | flops 443547648 | bytes 64499712 | tf_op jit(solution)/shard_map/convert_element_type | solution.py:65
  477.5 17.3 fusion.219
  504.6 19.2 %fusion.220 = (bf16[3072]{0:T(1024)(128)(2,1)}, bf16[8,128,3072]{2,1,0:T(8,128)(2,1)}) fusion(f32[8,128,3072]{2,1,0:T(8,128)} %get-tuple-element.203, bf16[8,128,768]{2,1,0:T(8,128)(2,1)} %get-tuple-element.173, bf16[2,3072,768]{2,1,0:T(8,128)(2,1)} %all-gather.18.cloned.1.call-done, f32[8,128,3072]{2,1,0:T(8,128)} %get-tuple-element.267, ...), kind=kOutput, calls=%fused_computation.536 | convolution fusion | flops 4882166784 | bytes 37767168 | tf_op jit(solution)/shard_map/gld,fd->glf/dot_general | solution.py:111
  638.2 18.4 %copy.400 = bf16[2,768,2304]{2,0,1:T(2,128)(2,1)} copy(bf16[2,768,2304]{1,2,0:T(8,128)(2,1)} %pad_maximum_fusion.5) | data formatting | bytes 14155776 | tf_op jit(solution)/shard_map/stack | solution.py:305
  667.4 18.3 %copy.397 = bf16[2,768,2304]{2,0,1:T(2,128)(2,1)} copy(bf16[2,768,2304]{1,2,0:T(8,128)(2,1)} %pad_maximum_fusion.4) | data formatting | bytes 14155776 | tf_op jit(solution)/shard_map/stack | solution.py:305
  800.4 74.9 %all-reduce.10.cloned.1.call-done = (bf16[2,768,2304]{2,0,1:T(2,128)(2,1)}, bf16[2,768,2304]{2,0,1:T(2,128)(2,1)}) async-done(((bf16[2,768,2304]{2,0,1:T(2,128)(2,1)}, bf16[2,768,2304]{2,0,1:T(2,128)(2,1)}), (bf16[2,768,2304]{2,0,1:T(2,128)(2,1)}, bf16[2,768,2304]{2,0,1:T(2,128)(2,1)})) %all-reduce.10.cloned.1.call-update) | async-done | bytes 14155792
  877.1 47.8 %copy.434 = bf16[2,96,2304]{0,1,2:T(8,128)(2,1)} copy(bf16[2,96,2304]{2,0,1:T(2,128)(2,1)S(1)} %constant_dynamic-slice_fusion.1) | data formatting | bytes 1769472
  924.8 83.7 %reshape.972 = bf16[2304,192]{1,0:T(8,128)(2,1)} reshape(bf16[2304,96,2]{2,1,0:T(8,128)(2,1)} %bitcast.442) | data formatting | bytes 1769472
  1010.4 47.8 %copy.436 = bf16[2,96,2304]{0,1,2:T(8,128)(2,1)} copy(bf16[2,96,2304]{2,0,1:T(2,128)(2,1)S(1)} %constant_dynamic-slice_fusion) | data formatting | bytes 1769472
  1058.2 83.7 %reshape.974 = bf16[2304,192]{1,0:T(8,128)(2,1)} reshape(bf16[2304,96,2]{2,1,0:T(8,128)(2,1)} %bitcast.443) | data formatting | bytes 1769472
  1164.1 31.9 %reduce-scatter.49.cloned.1.call-done = bf16[2,96,3072]{2,1,0:T(8,128)(2,1)} async-done(((bf16[2,768,3072]{2,1,0:T(8,128)(2,1)}), bf16[2,96,3072]{2,1,0:T(8,128)(2,1)}) %reduce-scatter.49.cloned.1.call-update) | async-done | bytes 1179664 | tf_op jit(solution)/shard_map/reduce_scatter | solution.py:344
  1216.8 16.4 reduce-scatter.71.cloned.1.call-done
  1234.1 36.2 %reduce-scatter.69.cloned.1.call-done = bf16[96,4]{1,0:T(8,128)(2,1)} async-done(((bf16[768,4]{1,0:T(8,128)(2,1)}), bf16[96,4]{1,0:T(8,128)(2,1)}) %reduce-scatter.69.cloned.1.call-update) | async-done | bytes 784
  1271.2 37.0 %reduce-scatter.79.cloned.1.call-done = bf16[384,2]{1,0:T(8,128)(2,1)} async-done(((bf16[3072,2]{1,0:T(8,128)(2,1)}), bf16[384,2]{1,0:T(8,128)(2,1)}) %reduce-scatter.79.cloned.1.call-update) | async-done | bytes 1552
  1309.2 37.0 %reduce-scatter.77.cloned.1.call-done = bf16[384,2]{1,0:T(8,128)(2,1)} async-done(((bf16[3072,2]{1,0:T(8,128)(2,1)}), bf16[384,2]{1,0:T(8,128)(2,1)}) %reduce-scatter.77.cloned.1.call-update) | async-done | bytes 1552
  1347.2 35.6 %reduce-scatter.75.cloned.1.call-done = bf16[96,12]{1,0:T(8,128)(2,1)} async-done(((bf16[768,12]{1,0:T(8,128)(2,1)}), bf16[96,12]{1,0:T(8,128)(2,1)}) %reduce-scatter.75.cloned.1.call-update) | async-done | bytes 2320
  1383.8 35.8 %reduce-scatter.73.cloned.1.call-done = bf16[96,12]{1,0:T(8,128)(2,1)} async-done(((bf16[768,12]{1,0:T(8,128)(2,1)}), bf16[96,12]{1,0:T(8,128)(2,1)}) %reduce-scatter.73.cloned.1.call-update) | async-done | bytes 2320
  1420.4 35.6 %reduce-scatter.81.cloned.1.call-done = bf16[96,64]{1,0:T(8,128)(2,1)} async-done(((bf16[768,64]{1,0:T(8,128)(2,1)}), bf16[96,64]{1,0:T(8,128)(2,1)}) %reduce-scatter.81.cloned.1.call-update) | async-done | bytes 12304
  1456.9 35.9 %reduce-scatter.83.cloned.1.call-done = bf16[96,64]{1,0:T(8,128)(2,1)} async-done(((bf16[768,64]{1,0:T(8,128)(2,1)}), bf16[96,64]{1,0:T(8,128)(2,1)}) %reduce-scatter.83.cloned.1.call-update) | async-done | bytes 12304
  1493.6 20.4 %all-reduce.4 = (f32[2,96,2]{1,2,0:T(2,128)}, f32[2,96,6]{1,2,0:T(8,128)S(1)}, f32[2,384]{1,0:T(2,128)}, f32[96,64]{0,1:T(8,128)}) all-reduce(f32[2,96,2]{1,2,0:T(2,128)S(1)} %convert_add_fusion.7, f32[2,96,6]{1,2,0:T(8,128)S(1)} %convert_add_fusion.5, f32[2,384]{1,0:T(2,128)S(1)} %convert_add_fusion.6, ...), channel_id=1, replica_groups=mesh['dp'=8,'seg'=4] {'seg'}, use_global_device_ids=true, to_apply=%region_65.66 | all-reduce | flops 8448 | bytes 67584 | tf_op jit(solution)/shard_map/psum | solution.py:309
  1517.8 20.9 %reduce-scatter.65.cloned.1.call-done = bf16[192,192]{1,0:T(8,128)(2,1)} async-done(((bf16[768,192]{1,0:T(8,128)(2,1)}), bf16[192,192]{1,0:T(8,128)(2,1)}) %reduce-scatter.65.cloned.1.call-update) | async-done | bytes 73744
  1540.6 27.9 %reduce-scatter.61.cloned.1.call-done = bf16[576,192]{1,0:T(8,128)(2,1)} async-done(((bf16[2304,192]{1,0:T(8,128)(2,1)}), bf16[576,192]{1,0:T(8,128)(2,1)}) %reduce-scatter.61.cloned.1.call-update) | async-done | bytes 221200
  1568.5 31.4 %reshape.973 = bf16[576,96,2]{2,1,0:T(8,128)(2,1)} reshape(bf16[576,192]{1,0:T(8,128)(2,1)} %reduce-scatter.61.cloned.1.call-done) | data formatting | bytes 442368
  1599.9 14.7 copy.435
  1614.6 31.4 %reshape.975 = bf16[576,96,2]{2,1,0:T(8,128)(2,1)} reshape(bf16[576,192]{1,0:T(8,128)(2,1)} %reduce-scatter.63.cloned.1.call-done) | data formatting | bytes 442368
  1645.9 14.6 copy.437
  1661.4 32.9 %all-reduce.12.cloned.1.call-done = (bf16[2,384,768]{1,0,2:T(2,128)(2,1)}, bf16[2,384,768]{1,0,2:T(2,128)(2,1)}) async-done(((bf16[2,384,768]{1,0,2:T(2,128)(2,1)}, bf16[2,384,768]{1,0,2:T(2,128)(2,1)}), (bf16[2,384,768]{1,0,2:T(2,128)(2,1)}, bf16[2,384,768]{1,0,2:T(2,128)(2,1)})) %all-reduce.12.cloned.1.call-update) | async-done | bytes 2359312
  1696.6 28.4 %reduce-scatter.55.cloned.1.call-done = bf16[2,96,768]{2,1,0:T(8,128)(2,1)} async-done(((bf16[2,96,3072]{2,1,0:T(8,128)(2,1)}), bf16[2,96,768]{2,1,0:T(8,128)(2,1)}) %reduce-scatter.55.cloned.1.call-update) | async-done | bytes 294928 | tf_op jit(solution)/shard_map/reduce_scatter | solution.py:343
  1724.9 30.3 %reduce-scatter.51.cloned.1.call-done = bf16[2,96,768]{2,1,0:T(8,128)(2,1)} async-done(((bf16[2,96,3072]{2,1,0:T(8,128)(2,1)}), bf16[2,96,768]{2,1,0:T(8,128)(2,1)}) %reduce-scatter.51.cloned.1.call-update) | async-done | bytes 294928 | tf_op jit(solution)/shard_map/reduce_scatter | solution.py:343
  (899 shorter events, 640.4 us)
Async XLA Ops:
  7.2 65.9 %all-gather.12.cloned.1.call-start = ((), (), s32[]{:S(2)}) async-start(), calls=%async_computation.22 | async-start | bytes 1474560 | tf_op jit(solution)/shard_map/all_gather | solution.py:230
  7.9 146.0 %all-gather.16.cloned.1.call-start = ((), (), s32[]{:S(2)}) async-start(), calls=%async_computation.24 | async-start | bytes 1474560 | tf_op jit(solution)/shard_map/all_gather | solution.py:233
  10.0 149.2 %all-gather.8.cloned.1.call-start = ((), (), s32[]{:S(2)}) async-start(), calls=%async_computation.20 | async-start | bytes 7962624 | tf_op jit(solution)/shard_map/all_gather | solution.py:223
  55.1 149.8 %all-gather.10.cloned.1.call-start = ((), (), s32[]{:S(2)}) async-start(), calls=%async_computation.21 | async-start | bytes 2654208 | tf_op jit(solution)/shard_map/all_gather | solution.py:226
  73.0 159.9 %all-gather.14.cloned.1.call-start = ((), (), s32[]{:S(2)}) async-start(), calls=%async_computation.23 | async-start | bytes 10616832 | tf_op jit(solution)/shard_map/all_gather | solution.py:229
  73.6 251.4 %all-gather.18.cloned.1.call-start = ((), (), s32[]{:S(2)}) async-start(), calls=%async_computation.25 | async-start | bytes 10616832 | tf_op jit(solution)/shard_map/all_gather | solution.py:232
  148.4 187.0 %copy-start.196 = (f32[768]{0:T(1024)}, f32[768]{0:T(1024)S(1)}, u32[]{:S(2)}) copy-start(f32[768]{0:T(1024)S(1)} %get-tuple-element.156) | copy-start | bytes 9220
  150.3 191.2 %copy-start.110 = (f32[768]{0:T(1024)}, f32[768]{0:T(1024)S(1)}, u32[]{:S(2)}) copy-start(f32[768]{0:T(1024)S(1)} %get-tuple-element.130) | copy-start | bytes 9220
  150.4 220.8 %copy-start.177 = (s32[2,16]{1,0:T(2,128)}, s32[2,16]{1,0:T(2,128)S(1)}, u32[]{:S(2)}) copy-start(s32[2,16]{1,0:T(2,128)S(1)} %get-tuple-element.253) | copy-start | bytes 388
  150.4 225.3 %copy-start.175 = (s32[2,16]{1,0:T(2,128)}, s32[2,16]{1,0:T(2,128)S(1)}, u32[]{:S(2)}) copy-start(s32[2,16]{1,0:T(2,128)S(1)} %get-tuple-element.254) | copy-start | bytes 388
  158.9 635.3 %reduce-scatter.47.cloned.1.call-start = ((), (), s32[]{:S(2)}) async-start(), calls=%async_computation.27 | async-start | bytes 2654208 | tf_op jit(solution)/shard_map/reduce_scatter | solution.py:336
  563.9 232.9 %reduce-scatter.45.cloned.1.call-start = ((), (), s32[]{:S(2)}) async-start(), calls=%async_computation.26 | async-start | bytes 2654208 | tf_op jit(solution)/shard_map/reduce_scatter | solution.py:336
  618.4 256.9 %all-reduce.10.cloned.1.call-start = ((), (), s32[]{:S(2)}) async-start(), calls=%async_computation.46 | async-start | bytes 28311552
  685.8 456.2 %reduce-scatter.59.cloned.1.call-start = ((), (), s32[]{:S(2)}) async-start(), calls=%async_computation.33 | async-start | bytes 10616832 | tf_op jit(solution)/shard_map/reduce_scatter | solution.py:352
  710.4 436.5 %reduce-scatter.57.cloned.1.call-start = ((), (), s32[]{:S(2)}) async-start(), calls=%async_computation.32 | async-start | bytes 10616832 | tf_op jit(solution)/shard_map/reduce_scatter | solution.py:352
  734.4 417.3 %reduce-scatter.53.cloned.1.call-start = ((), (), s32[]{:S(2)}) async-start(), calls=%async_computation.30 | async-start | bytes 10616832 | tf_op jit(solution)/shard_map/reduce_scatter | solution.py:344
  758.1 437.9 %reduce-scatter.49.cloned.1.call-start = ((), (), s32[]{:S(2)}) async-start(), calls=%async_computation.28 | async-start | bytes 10616832 | tf_op jit(solution)/shard_map/reduce_scatter | solution.py:344
  781.5 451.6 %reduce-scatter.71.cloned.1.call-start = ((), (), s32[]{:S(2)}) async-start(), calls=%async_computation.39 | async-start | bytes 221184
  783.9 486.4 %reduce-scatter.69.cloned.1.call-start = ((), (), s32[]{:S(2)}) async-start(), calls=%async_computation.38 | async-start | bytes 221184
  785.3 522.9 %reduce-scatter.79.cloned.1.call-start = ((), (), s32[]{:S(2)}) async-start(), calls=%async_computation.43 | async-start | bytes 884736
  786.8 559.4 %reduce-scatter.77.cloned.1.call-start = ((), (), s32[]{:S(2)}) async-start(), calls=%async_computation.42 | async-start | bytes 884736
  788.5 594.4 %reduce-scatter.75.cloned.1.call-start = ((), (), s32[]{:S(2)}) async-start(), calls=%async_computation.41 | async-start | bytes 221184
  790.2 629.3 %reduce-scatter.73.cloned.1.call-start = ((), (), s32[]{:S(2)}) async-start(), calls=%async_computation.40 | async-start | bytes 221184
  791.6 664.4 %reduce-scatter.81.cloned.1.call-start = ((), (), s32[]{:S(2)}) async-start(), calls=%async_computation.44 | async-start | bytes 221184
  792.9 699.8 %reduce-scatter.83.cloned.1.call-start = ((), (), s32[]{:S(2)}) async-start(), calls=%async_computation.45 | async-start | bytes 221184
  794.2 722.5 %reduce-scatter.67.cloned.1.call-start = ((), (), s32[]{:S(2)}) async-start(), calls=%async_computation.37 | async-start | bytes 491520
  796.8 742.0 %reduce-scatter.65.cloned.1.call-start = ((), (), s32[]{:S(2)}) async-start(), calls=%async_computation.36 | async-start | bytes 491520
  799.1 769.4 %reduce-scatter.61.cloned.1.call-start = ((), (), s32[]{:S(2)}) async-start(), calls=%async_computation.34 | async-start | bytes 1474560
  1008.6 606.0 %reduce-scatter.63.cloned.1.call-start = ((), (), s32[]{:S(2)}) async-start(), calls=%async_computation.35 | async-start | bytes 1474560
  1141.9 552.4 %all-reduce.12.cloned.1.call-start = ((), (), s32[]{:S(2)}) async-start(), calls=%async_computation.47 | async-start | bytes 4718592
  1151.6 573.3 %reduce-scatter.55.cloned.1.call-start = ((), (), s32[]{:S(2)}) async-start(), calls=%async_computation.31 | async-start | bytes 1474560 | tf_op jit(solution)/shard_map/reduce_scatter | solution.py:343
  1152.2 602.9 %reduce-scatter.51.cloned.1.call-start = ((), (), s32[]{:S(2)}) async-start(), calls=%async_computation.29 | async-start | bytes 1474560 | tf_op jit(solution)/shard_map/reduce_scatter | solution.py:343
  (227 other events, 2432.5 us)
Sparse Core Ops, SparseCore 0:
  9.6 46.6 all-gather.11
  58.4 31.0 all-gather.15
  91.9 49.1 all-gather.7
  143.5 28.8 all-gather.9
  174.1 58.6 all-gather.13
  234.6 58.6 all-gather.17
  564.0 42.2 reduce-scatter.46
  618.5 42.4 reduce-scatter.44
  685.9 189.3 all-reduce.9
  878.6 76.7 reduce-scatter.58
  959.0 76.6 reduce-scatter.56
  1039.1 76.6 reduce-scatter.52
  1119.3 76.6 reduce-scatter.48
  1199.5 33.6 reduce-scatter.70
  1236.6 33.6 reduce-scatter.68
  1273.3 34.9 reduce-scatter.78
  1311.3 34.9 reduce-scatter.76
  1349.1 33.6 reduce-scatter.74
  1385.9 33.6 reduce-scatter.72
  1422.4 33.6 reduce-scatter.80
  1459.1 33.6 reduce-scatter.82
  1495.6 21.0 reduce-scatter.66
  1519.6 19.1 reduce-scatter.64
  1540.9 27.5 reduce-scatter.60
  1570.8 27.9 reduce-scatter.62
  1601.0 93.2 all-reduce.11
  1696.5 28.3 reduce-scatter.54
  1727.2 27.9 reduce-scatter.50
where the time goes:
time: 1770 us; the launch traced here: 1760 us
  local copies, waits for them, and re-layouts  541 us (31%)
  waiting for transfers between devices  534 us (30%)
  matrix products  322 us (18%)
  other arithmetic  175 us (10%)
  blocking collectives  171 us (10%)
  between operations  19.8 us (1%)
    unnamed x42, waiting for transfers between devices  430 us
    unnamed x521, local copies, waits for them, and re-layouts  424 us
    convert_element_type x1, other arithmetic, block_forward(): activation = gelu_exact(pre_gelu).astype(jnp.bfloat16)  61.2 us
    reduce_scatter x2, waiting for transfers between devices, shards(): lax.psum_scatter(lax.psum_scatter(gradients[2].astype(jnp.bfloat16), 'dp'...  58.6 us
    another operation x16, other arithmetic, shards(): jnp.stack([local_term, cross_term * first_shard])  44.5 us
    all_gather x1, blocking collectives, shards(): lax.all_gather(project_in, 'seg', axis=2, tiled=True)  41.5 us
    dot_general x4, matrix products, block_backward(): jnp.einsum('gld,fd->glf', branch_grad, down_weight, preferred_element_typ...  41.3 us
    another operation x4, local copies, waits for them, and re-layouts, shards(): jnp.stack([local_term, cross_term * first_shard])  36.7 us
  transfers between devices with their start and end apart: 28, of which 17 were waited for; matrix products, arithmetic and copies ran while one was open for 45% of the time, Pallas kernels for 0%

commit v1 on v0

--- a/solution.py
+++ b/solution.py
@@ -9,6 +9,27 @@
 POS = 64
 NORM_EPS = 1e-05
 PRECISE = lax.Precision.HIGHEST
+
+
+def collect(shard, axis, dim):
+    peers, place, rows = (lax.axis_size(axis), lax.axis_index(axis), shard.shape[dim])
+    ahead = [(i, (i + 1) % peers) for i in range(peers)]
+    downward = [(i, (i - 1) % peers) for i in range(peers)]
+    out = jnp.zeros((*shard.shape[:dim], peers * rows, *shard.shape[dim + 1 :]), shard.dtype)
+    out = lax.dynamic_update_slice_in_dim(out, shard, place * rows, axis=dim)
+    from_left = from_right = shard
+    halfway = peers // 2
+    for step in range(1, halfway + 1):
+        from_left = lax.ppermute(from_left, axis, ahead)
+        out = lax.dynamic_update_slice_in_dim(
+            out, from_left, (place - step) % peers * rows, axis=dim
+        )
+        if step < peers - halfway:
+            from_right = lax.ppermute(from_right, axis, downward)
+            out = lax.dynamic_update_slice_in_dim(
+                out, from_right, (place + step) % peers * rows, axis=dim
+            )
+    return out
 
 
 def norm_apply(inputs, norm_gain, norm_shift):
@@ -220,9 +241,7 @@
     totals = None
     for micro_step in range(micro_count):
         weights = (
-            lax.all_gather(
-                lax.all_gather(project_in, "seg", axis=2, tiled=True), "dp", axis=1, tiled=True
-            ),
+            collect(lax.all_gather(project_in, "seg", axis=2, tiled=True), "dp", 1),
             lax.all_gather(
                 lax.all_gather(project_out, "seg", axis=2, tiled=True), "dp", axis=1, tiled=True
             ),

time: 1770 us -> 1990 us (1.12)
  local copies, waits for them, and re-layouts: 541 us -> 681 us
  matrix products: 322 us -> 346 us
    dynamic_update_slice x0 -> x8, local copies, waits for them, and re-layouts: none -> 116 us  [the longest x4 57.8 us: collect(): lax.dynamic_update_slice_in_dim(out, from_left, (place - step) % peers *...]
    ppermute x0 -> x7, waiting for transfers between devices: none -> 24.8 us  [the longest x3 24 us: collect(): from_right = lax.ppermute(from_right, axis, downward)]
    unnamed x521 -> x511, local copies, waits for them, and re-layouts: 424 us -> 407 us
  transfers between devices with their start and end apart: 28 -> 35, of which waited for: 17 -> 18; matrix products, arithmetic and copies ran while one was open for 45% -> 50% of each run, Pallas kernels for 0% -> 0%
where the time goes in v1:
time: 1990 us; the launch traced here: 1970 us
  local copies, waits for them, and re-layouts  681 us (34%)
  waiting for transfers between devices  540 us (27%)
  matrix products  346 us (17%)
  blocking collectives  190 us (10%)
  other arithmetic  181 us (9%)
    unnamed x42, waiting for transfers between devices  426 us
    unnamed x511, local copies, waits for them, and re-layouts  407 us
    convert_element_type x1, other arithmetic, block_forward(): activation = gelu_exact(pre_gelu).astype(jnp.bfloat16)  61.4 us
    reduce_scatter x2, waiting for transfers between devices, shards(): lax.psum_scatter(lax.psum_scatter(gradients[2].astype(jnp.bfloat16), 'dp'...  58.6 us
    dynamic_update_slice x4, local copies, waits for them, and re-layouts, collect(): lax.dynamic_update_slice_in_dim(out, from_left, (place - step) % peers *...  57.8 us
    dynamic_update_slice x3, local copies, waits for them, and re-layouts, collect(): lax.dynamic_update_slice_in_dim(out, from_right, (place + step) % peers *...  45.4 us
    another operation x16, other arithmetic, shards(): jnp.stack([local_term, cross_term * first_shard])  44.5 us
    dot_general x4, matrix products, block_backward(): jnp.einsum('gld,fd->glf', branch_grad, down_weight, preferred_element_typ...  41.7 us
  transfers between devices with their start and end apart: 35, of which 18 were waited for; matrix products, arithmetic and copies ran while one was open for 50% of the time, Pallas kernels for 0%

profile of v1, /device:TPU:0, one launch (start us, length us, event | category | flops | bytes accessed | tf_op | source)
XLA Modules:
  0.0 1968.3 jit_solution(17414852707030083559)
XLA Ops:
  11.0 19.4 all_gather.34
  32.7 31.8 %all_gather.32 = bf16[2,96,2304]{1,2,0:T(8,128)(2,1)S(1)} all-gather(bf16[2,96,576]{1,2,0:T(8,128)(2,1)S(1)} %copy.334), channel_id=1, replica_groups=mesh['dp'=8,'seg'=4] {'seg'}, dimensions={2}, use_global_device_ids=true | all-gather | bytes 1105920 | tf_op jit(solution)/shard_map/all_gather | solution.py:244
  71.1 24.3 %all_gather.33 = bf16[2,768,6]{2,0,1:T(2,128)(2,1)S(1)} all-gather(bf16[2,96,6]{2,0,1:T(2,128)(2,1)S(1)} %copy.344), channel_id=1, replica_groups=mesh['dp'=8,'seg'=4] {'dp'}, dimensions={1}, use_global_device_ids=true | all-gather | bytes 20736 | tf_op jit(solution)/shard_map/all_gather | solution.py:255
  118.9 17.8 all-gather
  197.2 24.0 %collective-permute-done.3 = bf16[2,96,2304]{2,1,0:T(8,128)(2,1)} collective-permute-done((bf16[2,96,2304]{2,1,0:T(8,128)(2,1)}, bf16[2,96,2304]{2,1,0:T(8,128)(2,1)}, u32[]{:S(2)}, u32[]{:S(2)}) %collective-permute-start.3) | collective-permute-done | bytes 884768 | tf_op jit(solution)/shard_map/ppermute | solution.py:28
  412.7 19.6 fusion.38
  432.4 61.4 %multiply_convert_fusion.1 = (bf16[8,128,3072]{2,1,0:T(8,128)(2,1)}, f32[8,128,3072]{2,1,0:T(8,128)}, bf16[8,128,3072]{2,1,0:T(8,128)(2,1)}, f32[8,128,3072]{2,1,0:T(8,128)}) fusion(f32[8,128,3072]{2,1,0:T(8,128)} %get-tuple-element.269, f32[3072]{0:T(1024)S(1)} %bitcast.516, u8[128,3072]{1,0:T(8,128)(4,1)S(1)} %get-tuple-element.109, ...), kind=kLoop, calls=%fused_computation.28 | loop fusion | flops 443547648 | bytes 64499712 | tf_op jit(solution)/shard_map/convert_element_type | solution.py:86
  661.6 17.8 fusion.218
  689.2 19.1 fusion.219
  812.7 18.4 copy.414
  873.3 18.3 copy.417
  1007.0 72.6 %all-reduce.10.cloned.1.call-done = (bf16[2,768,2304]{2,0,1:T(2,128)(2,1)}, bf16[2,768,2304]{2,0,1:T(2,128)(2,1)}) async-done(((bf16[2,768,2304]{2,0,1:T(2,128)(2,1)}, bf16[2,768,2304]{2,0,1:T(2,128)(2,1)}), (bf16[2,768,2304]{2,0,1:T(2,128)(2,1)}, bf16[2,768,2304]{2,0,1:T(2,128)(2,1)})) %all-reduce.10.cloned.1.call-update) | async-done | bytes 14155792
  1081.4 47.8 %copy.457 = bf16[2,96,2304]{0,1,2:T(8,128)(2,1)} copy(bf16[2,96,2304]{2,0,1:T(2,128)(2,1)S(1)} %constant_dynamic-slice_fusion) | data formatting | bytes 1769472
  1129.2 83.7 %reshape.977 = bf16[2304,192]{1,0:T(8,128)(2,1)} reshape(bf16[2304,96,2]{2,1,0:T(8,128)(2,1)} %bitcast.450) | data formatting | bytes 1769472
  1214.8 47.8 %copy.455 = bf16[2,96,2304]{0,1,2:T(8,128)(2,1)} copy(bf16[2,96,2304]{2,0,1:T(2,128)(2,1)S(1)} %constant_dynamic-slice_fusion.1) | data formatting | bytes 1769472
  1262.5 83.7 %reshape.975 = bf16[2304,192]{1,0:T(8,128)(2,1)} reshape(bf16[2304,96,2]{2,1,0:T(8,128)(2,1)} %bitcast.451) | data formatting | bytes 1769472
  1369.6 30.7 %reduce-scatter.53.cloned.1.call-done = bf16[2,96,3072]{2,1,0:T(8,128)(2,1)} async-done(((bf16[2,768,3072]{2,1,0:T(8,128)(2,1)}), bf16[2,96,3072]{2,1,0:T(8,128)(2,1)}) %reduce-scatter.53.cloned.1.call-update) | async-done | bytes 1179664 | tf_op jit(solution)/shard_map/reduce_scatter | solution.py:363
  1438.3 36.2 %reduce-scatter.71.cloned.1.call-done = bf16[96,4]{1,0:T(8,128)(2,1)} async-done(((bf16[768,4]{1,0:T(8,128)(2,1)}), bf16[96,4]{1,0:T(8,128)(2,1)}) %reduce-scatter.71.cloned.1.call-update) | async-done | bytes 784
  1475.4 37.0 %reduce-scatter.77.cloned.1.call-done = bf16[384,2]{1,0:T(8,128)(2,1)} async-done(((bf16[3072,2]{1,0:T(8,128)(2,1)}), bf16[384,2]{1,0:T(8,128)(2,1)}) %reduce-scatter.77.cloned.1.call-update) | async-done | bytes 1552
  1513.5 37.0 %reduce-scatter.79.cloned.1.call-done = bf16[384,2]{1,0:T(8,128)(2,1)} async-done(((bf16[3072,2]{1,0:T(8,128)(2,1)}), bf16[384,2]{1,0:T(8,128)(2,1)}) %reduce-scatter.79.cloned.1.call-update) | async-done | bytes 1552
  1551.4 35.6 %reduce-scatter.73.cloned.1.call-done = bf16[96,12]{1,0:T(8,128)(2,1)} async-done(((bf16[768,12]{1,0:T(8,128)(2,1)}), bf16[96,12]{1,0:T(8,128)(2,1)}) %reduce-scatter.73.cloned.1.call-update) | async-done | bytes 2320
  1587.9 35.8 %reduce-scatter.75.cloned.1.call-done = bf16[96,12]{1,0:T(8,128)(2,1)} async-done(((bf16[768,12]{1,0:T(8,128)(2,1)}), bf16[96,12]{1,0:T(8,128)(2,1)}) %reduce-scatter.75.cloned.1.call-update) | async-done | bytes 2320
  1624.6 35.6 %reduce-scatter.83.cloned.1.call-done = bf16[96,64]{1,0:T(8,128)(2,1)} async-done(((bf16[768,64]{1,0:T(8,128)(2,1)}), bf16[96,64]{1,0:T(8,128)(2,1)}) %reduce-scatter.83.cloned.1.call-update) | async-done | bytes 12304
  1661.0 35.9 %reduce-scatter.81.cloned.1.call-done = bf16[96,64]{1,0:T(8,128)(2,1)} async-done(((bf16[768,64]{1,0:T(8,128)(2,1)}), bf16[96,64]{1,0:T(8,128)(2,1)}) %reduce-scatter.81.cloned.1.call-update) | async-done | bytes 12304
  1697.7 21.1 %all-reduce.4 = (f32[2,96,2]{1,2,0:T(2,128)}, f32[2,96,6]{1,2,0:T(8,128)S(1)}, f32[2,384]{1,0:T(2,128)}, f32[96,64]{0,1:T(8,128)}) all-reduce(f32[2,96,2]{1,2,0:T(2,128)S(1)} %convert_add_fusion.7, f32[2,96,6]{1,2,0:T(8,128)S(1)} %convert_add_fusion.5, f32[2,384]{1,0:T(2,128)S(1)} %convert_add_fusion.6, ...), channel_id=1, replica_groups=mesh['dp'=8,'seg'=4] {'seg'}, use_global_device_ids=true, to_apply=%region_65.66 | all-reduce | flops 8448 | bytes 67584 | tf_op jit(solution)/shard_map/psum | solution.py:328
  1722.1 20.5 %reduce-scatter.67.cloned.1.call-done = bf16[192,192]{1,0:T(8,128)(2,1)} async-done(((bf16[768,192]{1,0:T(8,128)(2,1)}), bf16[192,192]{1,0:T(8,128)(2,1)}) %reduce-scatter.67.cloned.1.call-update) | async-done | bytes 73744
  1744.4 28.0 %reduce-scatter.63.cloned.1.call-done = bf16[576,192]{1,0:T(8,128)(2,1)} async-done(((bf16[2304,192]{1,0:T(8,128)(2,1)}), bf16[576,192]{1,0:T(8,128)(2,1)}) %reduce-scatter.63.cloned.1.call-update) | async-done | bytes 221200
  1772.4 31.4 %reshape.978 = bf16[576,96,2]{2,1,0:T(8,128)(2,1)} reshape(bf16[576,192]{1,0:T(8,128)(2,1)} %reduce-scatter.63.cloned.1.call-done) | data formatting | bytes 442368
  1818.5 31.4 %reshape.976 = bf16[576,96,2]{2,1,0:T(8,128)(2,1)} reshape(bf16[576,192]{1,0:T(8,128)(2,1)} %reduce-scatter.61.cloned.1.call-done) | data formatting | bytes 442368
  1865.3 32.9 %all-reduce.12.cloned.1.call-done = (bf16[2,384,768]{1,0,2:T(2,128)(2,1)}, bf16[2,384,768]{1,0,2:T(2,128)(2,1)}) async-done(((bf16[2,384,768]{1,0,2:T(2,128)(2,1)}, bf16[2,384,768]{1,0,2:T(2,128)(2,1)}), (bf16[2,384,768]{1,0,2:T(2,128)(2,1)}, bf16[2,384,768]{1,0,2:T(2,128)(2,1)})) %all-reduce.12.cloned.1.call-update) | async-done | bytes 2359312
  1900.5 28.3 %reduce-scatter.51.cloned.1.call-done = bf16[2,96,768]{2,1,0:T(8,128)(2,1)} async-done(((bf16[2,96,3072]{2,1,0:T(8,128)(2,1)}), bf16[2,96,768]{2,1,0:T(8,128)(2,1)}) %reduce-scatter.51.cloned.1.call-update) | async-done | bytes 294928 | tf_op jit(solution)/shard_map/reduce_scatter | solution.py:362
  1928.8 30.3 %reduce-scatter.55.cloned.1.call-done = bf16[2,96,768]{2,1,0:T(8,128)(2,1)} async-done(((bf16[2,96,3072]{2,1,0:T(8,128)(2,1)}), bf16[2,96,768]{2,1,0:T(8,128)(2,1)}) %reduce-scatter.55.cloned.1.call-update) | async-done | bytes 294928 | tf_op jit(solution)/shard_map/reduce_scatter | solution.py:362
  (912 shorter events, 833.5 us)
Async XLA Ops:
  7.2 59.3 %all-gather.10.cloned.1.call-start = ((), (), s32[]{:S(2)}) async-start(), calls=%async_computation.21 | async-start | bytes 1474560 | tf_op jit(solution)/shard_map/all_gather | solution.py:249
  7.9 252.1 %all-gather.14.cloned.1.call-start = ((), (), s32[]{:S(2)}) async-start(), calls=%async_computation.23 | async-start | bytes 1474560 | tf_op jit(solution)/shard_map/all_gather | solution.py:252
  10.0 370.4 %all-gather.8.cloned.1.call-start = ((), (), s32[]{:S(2)}) async-start(), calls=%async_computation.20 | async-start | bytes 2654208 | tf_op jit(solution)/shard_map/all_gather | solution.py:245
  31.5 355.1 %all-gather.18.cloned.1.call-start = ((), (), s32[]{:S(2)}) async-start(), calls=%async_computation.25 | async-start | bytes 7962624 | tf_op jit(solution)/shard_map/all_gather | solution.py:284
  66.4 335.7 %all-gather.12.cloned.1.call-start = ((), (), s32[]{:S(2)}) async-start(), calls=%async_computation.22 | async-start | bytes 10616832 | tf_op jit(solution)/shard_map/all_gather | solution.py:248
  67.0 426.8 %all-gather.16.cloned.1.call-start = ((), (), s32[]{:S(2)}) async-start(), calls=%async_computation.24 | async-start | bytes 10616832 | tf_op jit(solution)/shard_map/all_gather | solution.py:251
  68.4 124.2 %collective-permute-start.1 = (bf16[2,96,2304]{2,1,0:T(8,128)(2,1)}, bf16[2,96,2304]{2,1,0:T(8,128)(2,1)}, u32[]{:S(2)}, u32[]{:S(2)}) collective-permute-start(bf16[2,96,2304]{2,1,0:T(8,128)(2,1)} %copy.335), channel_id=1, source_target_pairs={{0,28},{4,0},{8,4},{12,8},{16,12},{20,16},{24,20},{28,24},{1,29},{... | collective-permute-start | bytes 2654216 | tf_op jit(solution)/shard_map/ppermute | solution.py:28
  118.5 74.1 %collective-permute-start.2 = (bf16[2,96,2304]{2,1,0:T(8,128)(2,1)}, bf16[2,96,2304]{2,1,0:T(8,128)(2,1)}, u32[]{:S(2)}, u32[]{:S(2)}) collective-permute-start(bf16[2,96,2304]{2,1,0:T(8,128)(2,1)} %collective-permute-done), channel_id=1, source_target_pairs={{0,4},{4,8},{8,12},{12,16},{16,20},{20,24},{24,28},{28,0},{1,5},{5... | collective-permute-start | bytes 2654216 | tf_op jit(solution)/shard_map/ppermute | solution.py:23
  221.2 96.8 %collective-permute-start.5 = (bf16[2,96,2304]{2,1,0:T(8,128)(2,1)}, bf16[2,96,2304]{2,1,0:T(8,128)(2,1)}, u32[]{:S(2)}, u32[]{:S(2)}) collective-permute-start(bf16[2,96,2304]{2,1,0:T(8,128)(2,1)} %collective-permute-done.3), channel_id=1, source_target_pairs={{0,28},{4,0},{8,4},{12,8},{16,12},{20,16},{24,20},{28,24},{1,29},{... | collective-permute-start | bytes 2654216 | tf_op jit(solution)/shard_map/ppermute | solution.py:28
  224.8 110.5 %collective-permute-start.6 = (bf16[2,96,2304]{2,1,0:T(8,128)(2,1)}, bf16[2,96,2304]{2,1,0:T(8,128)(2,1)}, u32[]{:S(2)}, u32[]{:S(2)}) collective-permute-start(bf16[2,96,2304]{2,1,0:T(8,128)(2,1)} %collective-permute-done.4), channel_id=1, source_target_pairs={{0,4},{4,8},{8,12},{12,16},{16,20},{20,24},{24,28},{28,0},{1,5},{5... | collective-permute-start | bytes 2654216 | tf_op jit(solution)/shard_map/ppermute | solution.py:23
  264.8 736.1 %reduce-scatter.45.cloned.1.call-start = ((), (), s32[]{:S(2)}) async-start(), calls=%async_computation.26 | async-start | bytes 2654208 | tf_op jit(solution)/shard_map/reduce_scatter | solution.py:355
  744.6 258.6 %reduce-scatter.47.cloned.1.call-start = ((), (), s32[]{:S(2)}) async-start(), calls=%async_computation.27 | async-start | bytes 2654208 | tf_op jit(solution)/shard_map/reduce_scatter | solution.py:355
  802.0 277.6 %all-reduce.10.cloned.1.call-start = ((), (), s32[]{:S(2)}) async-start(), calls=%async_computation.46 | async-start | bytes 28311552
  891.7 454.6 %reduce-scatter.57.cloned.1.call-start = ((), (), s32[]{:S(2)}) async-start(), calls=%async_computation.32 | async-start | bytes 10616832 | tf_op jit(solution)/shard_map/reduce_scatter | solution.py:371
  916.2 435.0 %reduce-scatter.59.cloned.1.call-start = ((), (), s32[]{:S(2)}) async-start(), calls=%async_computation.33 | async-start | bytes 10616832 | tf_op jit(solution)/shard_map/reduce_scatter | solution.py:371
  941.2 414.9 %reduce-scatter.49.cloned.1.call-start = ((), (), s32[]{:S(2)}) async-start(), calls=%async_computation.28 | async-start | bytes 10616832 | tf_op jit(solution)/shard_map/reduce_scatter | solution.py:363
  964.7 435.6 %reduce-scatter.53.cloned.1.call-start = ((), (), s32[]{:S(2)}) async-start(), calls=%async_computation.30 | async-start | bytes 10616832 | tf_op jit(solution)/shard_map/reduce_scatter | solution.py:363
  988.1 449.4 %reduce-scatter.69.cloned.1.call-start = ((), (), s32[]{:S(2)}) async-start(), calls=%async_computation.38 | async-start | bytes 221184
  990.3 484.3 %reduce-scatter.71.cloned.1.call-start = ((), (), s32[]{:S(2)}) async-start(), calls=%async_computation.39 | async-start | bytes 221184
  991.7 520.8 %reduce-scatter.77.cloned.1.call-start = ((), (), s32[]{:S(2)}) async-start(), calls=%async_computation.42 | async-start | bytes 884736
  993.1 557.3 %reduce-scatter.79.cloned.1.call-start = ((), (), s32[]{:S(2)}) async-start(), calls=%async_computation.43 | async-start | bytes 884736
  995.0 592.0 %reduce-scatter.73.cloned.1.call-start = ((), (), s32[]{:S(2)}) async-start(), calls=%async_computation.40 | async-start | bytes 221184
  996.8 626.8 %reduce-scatter.75.cloned.1.call-start = ((), (), s32[]{:S(2)}) async-start(), calls=%async_computation.41 | async-start | bytes 221184
  998.3 661.9 %reduce-scatter.83.cloned.1.call-start = ((), (), s32[]{:S(2)}) async-start(), calls=%async_computation.45 | async-start | bytes 221184
  999.6 697.3 %reduce-scatter.81.cloned.1.call-start = ((), (), s32[]{:S(2)}) async-start(), calls=%async_computation.44 | async-start | bytes 221184
  1000.8 720.2 %reduce-scatter.65.cloned.1.call-start = ((), (), s32[]{:S(2)}) async-start(), calls=%async_computation.36 | async-start | bytes 491520
  1003.2 739.4 %reduce-scatter.67.cloned.1.call-start = ((), (), s32[]{:S(2)}) async-start(), calls=%async_computation.37 | async-start | bytes 491520
  1005.5 766.9 %reduce-scatter.63.cloned.1.call-start = ((), (), s32[]{:S(2)}) async-start(), calls=%async_computation.35 | async-start | bytes 1474560
  1212.9 605.5 %reduce-scatter.61.cloned.1.call-start = ((), (), s32[]{:S(2)}) async-start(), calls=%async_computation.34 | async-start | bytes 1474560
  1346.3 552.0 %all-reduce.12.cloned.1.call-start = ((), (), s32[]{:S(2)}) async-start(), calls=%async_computation.47 | async-start | bytes 4718592
  1356.0 572.8 %reduce-scatter.51.cloned.1.call-start = ((), (), s32[]{:S(2)}) async-start(), calls=%async_computation.29 | async-start | bytes 1474560 | tf_op jit(solution)/shard_map/reduce_scatter | solution.py:362
  1356.6 602.5 %reduce-scatter.55.cloned.1.call-start = ((), (), s32[]{:S(2)}) async-start(), calls=%async_computation.31 | async-start | bytes 1474560 | tf_op jit(solution)/shard_map/reduce_scatter | solution.py:362
  (229 other events, 3849.5 us)
Sparse Core Ops, SparseCore 0:
  9.6 45.7 all-gather.9
  57.5 29.6 all-gather.13
  89.7 29.4 all-gather.7
  121.0 48.4 all-gather.17
  171.2 83.0 all-gather.11
  265.0 57.7 all-gather.15
  744.7 40.5 reduce-scatter.44
  802.2 40.9 reduce-scatter.46
  891.8 187.7 all-reduce.9
  1083.0 76.7 reduce-scatter.56
  1163.3 76.6 reduce-scatter.58
  1243.4 76.6 reduce-scatter.48
  1323.6 76.6 reduce-scatter.52
  1403.7 33.6 reduce-scatter.68
  1440.9 33.6 reduce-scatter.70
  1477.5 34.9 reduce-scatter.76
  1515.5 34.9 reduce-scatter.78
  1553.3 33.6 reduce-scatter.72
  1590.0 33.6 reduce-scatter.74
  1626.5 33.6 reduce-scatter.82
  1663.2 33.6 reduce-scatter.80
  1699.7 21.2 reduce-scatter.64
  1723.9 18.6 reduce-scatter.66
  1744.8 27.5 reduce-scatter.62
  1774.7 27.9 reduce-scatter.60
  1804.9 93.2 all-reduce.11
  1900.4 28.3 reduce-scatter.50
  1931.1 27.9 reduce-scatter.54
